TPU v7x, 32 devices: a whole 2x2x4 slice. The times are simulated.
32 devices in a mesh: blk: 4 (over z), virt: 8 (over y, x, core).
Axes of the slice: x: 2, y: 2, z: 4, core: 2. Of those that a mesh axis runs over, the one named last changes fastest.
Arguments:
- integrals: bfloat16 [512, 16, 4096], P(('blk', 'virt')), may hold values from -0.09375 to 0.09375
- amplitudes: bfloat16 [256, 4096], P('blk'), may hold values from -6 to 6
- readers: int32 [512], P(('blk', 'virt')), may hold values from 0 to 7, as said below
- row_slots: int32 [512], P(('blk', 'virt')), may hold values from 0 to 3
- tile_mask: int32 [512, 4], P(('blk', 'virt')), may hold values 0 or 1
- virt_energy: float32 [2048], P(('blk', 'virt')), may hold values from 1 to 3
- occ_energy: float32 [1200], replicated, may hold values from -1 to -0.25
- pair_first: int32 [256], replicated, may hold values from 0 to 1199
- pair_second: int32 [256], replicated, may hold values from 0 to 1199
Outputs:
- update: bfloat16 [2048, 256], P(('blk', 'virt'))
Inputs may be any that keep to these rules, and one draw needn't show every extreme that they name: `readers`: each tile names a reader on the virt axis in the same blk row as its generating device; one device names one reader at most 4 times, and in every blk row some reader is named 4 times by every device of that row.
All inputs are finite; a program needn't handle non-finite values. No bound on the sum of `tile_mask` on one device may be relied on, other than what follows from the above.
Results may differ from a plain program's by a relative error of at most 0.001.
Values may be sent and summed in bfloat16 or wider, within the bound.
A program may use at most 64 MiB of HBM per device.

v0:
```python
import jax
import jax.numpy as jnp
from jax import lax
from jax.sharding import PartitionSpec as P


def body(
    integrals,
    amplitudes,
    readers,
    row_slots,
    tile_mask,
    virt_energy,
    occ_energy,
    pair_first,
    pair_second,
):
    virt_count = lax.axis_size("virt")
    blk_count = lax.axis_size("blk")
    generated = integrals.shape[0]
    tile_rows = integrals.shape[1]
    panel_rows = amplitudes.shape[0]
    capacity = max(1, 2 * generated // virt_count)
    slot_count = virt_count * capacity
    row_blocks = virt_energy.shape[0] // tile_rows
    tile_order = jnp.arange(generated, dtype=jnp.int32)
    same_reader = readers[:, None] == readers[None, :]
    earlier = tile_order[None, :] < tile_order[:, None]
    within = jnp.sum((same_reader & earlier).astype(jnp.int32), axis=1)
    position = readers * capacity + within
    placing = jnp.arange(slot_count, dtype=jnp.int32)[:, None] == position[None, :]
    filled = jnp.any(placing, axis=1)
    source_tile = jnp.sum(placing.astype(jnp.int32) * tile_order[None, :], axis=1)
    row_hot = (row_slots[:, None] == jnp.arange(row_blocks, dtype=jnp.int32)[None, :]).astype(
        jnp.float32
    )
    mask_float = tile_mask.astype(jnp.float32)
    sent_tiles = jnp.where(
        filled[:, None, None], integrals[source_tile], jnp.zeros((), jnp.bfloat16)
    )
    coefficient = (row_hot[:, :, None] * mask_float[:, None, :]).reshape(
        generated, row_blocks * blk_count
    )
    sent_coef = jnp.where(filled[:, None], coefficient[source_tile], 0.0).astype(jnp.bfloat16)
    got_tiles, got_coef = (
        lax.all_to_all(sent_tiles, "virt", split_axis=0, concat_axis=0, tiled=True),
        lax.all_to_all(sent_coef, "virt", split_axis=0, concat_axis=0, tiled=True),
    )
    got_coef = got_coef.astype(jnp.float32).reshape(slot_count, row_blocks, blk_count)
    panel = lax.all_gather(amplitudes, "blk", axis=0, tiled=True)
    column_count = panel.shape[0]
    column_panel = jnp.arange(column_count, dtype=jnp.int32) // panel_rows
    columns = jnp.einsum(
        "srk,kp->srp",
        got_coef,
        (jnp.arange(blk_count, dtype=jnp.int32)[:, None] == column_panel[None, :]).astype(
            jnp.float32
        ),
        precision=lax.Precision.HIGHEST,
    )
    product = jnp.einsum("stw,pw->stp", got_tiles, panel, preferred_element_type=jnp.float32)
    summed_panel = jnp.einsum("srp,stp->rtp", columns, product, precision=lax.Precision.HIGHEST)
    summed = summed_panel.reshape(row_blocks * tile_rows, column_count)
    levels = jnp.arange(occ_energy.shape[0], dtype=jnp.int32)[None, :]
    first_energy = jnp.sum(
        jnp.where(pair_first[:, None] == levels, occ_energy[None, :], 0.0), axis=1
    )
    second_energy = jnp.sum(
        jnp.where(pair_second[:, None] == levels, occ_energy[None, :], 0.0), axis=1
    )
    denominator = virt_energy[:, None] - first_energy[None, :] - second_energy[None, :]
    return (summed / denominator).astype(jnp.bfloat16)


def solution(mesh):
    placed = (
        P(("blk", "virt"), None, None),
        P("blk", None),
        P(("blk", "virt")),
        P(("blk", "virt")),
        P(("blk", "virt"), None),
        P(("blk", "virt")),
        P(),
        P(),
        P(),
    )
    return jax.shard_map(
        body, mesh=mesh, in_specs=placed, out_specs=P(("blk", "virt"), None), check_vma=False
    )
```

profile of v0, /device:TPU:0, one launch (start us, length us, event | category | flops | bytes accessed | tf_op | source)
XLA Modules:
  0.0 97.9 jit_solution(15406979760878977125)
XLA Ops:
  6.5 0.0 copy-start
  6.5 1.0 %convert_reduce_fusion = s32[16]{0:T(128)S(1)} fusion(s32[16]{0:T(128)} %param.11), kind=kLoop, calls=%fused_computation.16 | loop fusion | flops 1264 | bytes 128 | tf_op jit(solution)/shard_map/reduce_sum | solution.py:29
  7.5 0.7 multiply_add_fusion
  8.2 0.1 select_reduce_fusion.2
  8.3 0.1 fusion.5
  8.4 0.7 convert_element_type.25
  9.1 0.7 fusion.10
  9.8 0.1 copy.20
  9.8 0.1 broadcast_in_dim.44
  9.9 0.6 gather_fusion.1
  10.5 0.7 select_convert_fusion
  11.2 5.2 %all-to-all-start.1 = ((bf16[8,4,16]{2,1,0:T(4,128)(2,1)}), bf16[8,4,16]{2,1,0:T(4,128)(2,1)S(1)}, u32[]{:S(2)}, u32[]{:S(2)}) async-start(bf16[8,4,16]{2,1,0:T(4,128)(2,1)} %select_convert_fusion), calls=%async_computation.1 | async-start | bytes 16384 | tf_op jit(solution)/shard_map/all_to_all | solution.py:47
  16.4 0.0 copy-done
  16.4 2.8 %gather_fusion = bf16[32,16,4096]{2,1,0:T(8,128)(2,1)} fusion(bf16[16,16,4096]{2,1,0:T(8,128)(2,1)S(1)} %copy-done, s32[1024]{0:T(1024)S(1)} %pad_clamp_fusion), kind=kCustom, calls=%fused_computation | custom fusion | bytes 8388736 | tf_op jit(solution)/shard_map/gather | solution.py:39
  19.2 4.5 %broadcast_select_fusion = bf16[32,16,4096]{2,1,0:T(8,128)(2,1)} fusion(bf16[32,16,4096]{2,1,0:T(8,128)(2,1)} %gather_fusion, pred[32]{0:T(512)(128)(4,1)S(1)} %fusion.5), kind=kLoop, calls=%fused_computation.2 | loop fusion | flops 2097152 | bytes 8388640 | tf_op jit(solution)/shard_map/jit(_where)/select_n | solution.py:38
  23.7 0.0 copy-start.1
  23.7 0.0 copy-start.2
  23.7 0.0 copy-start.3
  23.7 0.0 all-to-all-done.1
  23.7 4.7 %all-to-all-start = ((bf16[32,16,4096]{2,1,0:T(8,128)(2,1)}), bf16[32,16,4096]{2,1,0:T(8,128)(2,1)}, u32[]{:S(2)}, u32[]{:S(2)}) async-start(bf16[32,16,4096]{2,1,0:T(8,128)(2,1)} %broadcast_select_fusion), calls=%async_computation | async-start | bytes 8388608 | tf_op jit(solution)/shard_map/all_to_all | solution.py:46
  28.4 0.0 all-gather.2.cloned.1.call-start
  28.4 0.7 all-gather.2.cloned.1.call-update
  29.1 0.0 copy-done.1
  29.1 0.0 copy-done.2
  29.1 0.0 copy-done.3
  29.2 0.4 select_reduce_fusion.1
  29.5 0.1 reshape.99
  29.6 0.1 fusion.3
  29.8 0.2 copy.23
  30.0 48.4 %all-gather.2.cloned.1.call-done = bf16[256,4096]{1,0:T(8,128)(2,1)} async-done(((bf16[64,4096]{1,0:T(8,128)(2,1)}), bf16[256,4096]{1,0:T(8,128)(2,1)}) %all-gather.2.cloned.1.call-update) | async-done | bytes 2097168 | tf_op jit(solution)/shard_map/all_gather | solution.py:50
  78.4 0.0 all-to-all-done
  78.4 4.1 %fusion = f32[32,16,256]{2,1,0:T(8,128)S(1)} fusion(bf16[32,16,4096]{2,1,0:T(8,128)(2,1)} %all-to-all-done, bf16[256,4096]{1,0:T(8,128)(2,1)} %all-gather.2.cloned.1.call-done), kind=kOutput, calls=%fused_computation.3 | convolution fusion | flops 1073741824 | bytes 6815744 | tf_op jit(solution)/shard_map/stw,pw->stp/dot_general | solution.py:61
  82.6 2.6 %copy.22 = f32[32,16,256]{0,1,2:T(8,128)} copy(f32[32,16,256]{2,1,0:T(8,128)S(1)} %fusion) | data formatting | bytes 1048576 | tf_op jit(solution)/shard_map/stw,pw->stp/dot_general | solution.py:61
  85.2 0.0 copy-start.4
  85.2 5.0 %convolution_bitcast_fusion = f32[4,16,256]{1,0,2:T(4,128)S(1)} fusion(f32[32,16,256]{0,1,2:T(8,128)} %copy.22, f32[32,4,256]{0,1,2:T(4,128)S(1)} %copy.23), kind=kOutput, calls=%fused_computation.5 | convolution fusion | flops 6291456 | bytes 720896 | tf_op jit(solution)/shard_map/srp,stp->rtp/dot_general | solution.py:62
  90.2 0.2 copy.24
  90.4 0.0 copy-done.4
  90.4 0.7 fusion.2
  (4 shorter events, 0.0 us)
Async XLA Ops:
  6.5 9.8 %copy-start = (bf16[16,16,4096]{2,1,0:T(8,128)(2,1)S(1)}, bf16[16,16,4096]{2,1,0:T(8,128)(2,1)}, u32[]{:S(2)}) copy-start(bf16[16,16,4096]{2,1,0:T(8,128)(2,1)} %param.9) | copy-start | bytes 6291460
  11.2 12.5 %all-to-all-start.1 = ((bf16[8,4,16]{2,1,0:T(4,128)(2,1)}), bf16[8,4,16]{2,1,0:T(4,128)(2,1)S(1)}, u32[]{:S(2)}, u32[]{:S(2)}) async-start(bf16[8,4,16]{2,1,0:T(4,128)(2,1)} %select_convert_fusion), calls=%async_computation.1 | async-start | bytes 16384 | tf_op jit(solution)/shard_map/all_to_all | solution.py:47
  23.7 5.5 %copy-start.1 = (f32[1200]{0:T(1024)S(1)}, f32[1200]{0:T(1024)}, u32[]{:S(2)}) copy-start(f32[1200]{0:T(1024)} %param.15) | copy-start | bytes 14404
  23.7 5.5 %copy-start.2 = (s32[256]{0:T(256)S(1)}, s32[256]{0:T(256)}, u32[]{:S(2)}) copy-start(s32[256]{0:T(256)} %param.16) | copy-start | bytes 3076
  23.7 5.5 %copy-start.3 = (s32[256]{0:T(256)S(1)}, s32[256]{0:T(256)}, u32[]{:S(2)}) copy-start(s32[256]{0:T(256)} %param.17) | copy-start | bytes 3076
  23.7 54.8 %all-to-all-start = ((bf16[32,16,4096]{2,1,0:T(8,128)(2,1)}), bf16[32,16,4096]{2,1,0:T(8,128)(2,1)}, u32[]{:S(2)}, u32[]{:S(2)}) async-start(bf16[32,16,4096]{2,1,0:T(8,128)(2,1)} %broadcast_select_fusion), calls=%async_computation | async-start | bytes 8388608 | tf_op jit(solution)/shard_map/all_to_all | solution.py:46
  28.4 50.1 %all-gather.2.cloned.1.call-start = ((), (), s32[]{:S(2)}) async-start(), calls=%async_computation.2 | async-start | bytes 2621440 | tf_op jit(solution)/shard_map/all_gather | solution.py:50
  85.2 5.2 %copy-start.4 = (f32[64]{0:T(128)S(1)}, f32[64]{0:T(128)}, u32[]{:S(2)}) copy-start(f32[64]{0:T(128)} %param.14) | copy-start | bytes 772
Sparse Core Ops, SparseCore 0:
  30.8 47.6 all-gather.1
where the time goes:
time: 98.4 us; the launch traced here: 97.9 us
  waiting for transfers between devices  49.1 us (50%)
  between operations  13.5 us (14%)
  starting transfers between devices  9.9 us (10%)
  other arithmetic  9.47 us (10%)
  matrix products  9.28 us (9%)
  local copies, waits for them, and re-layouts  6.7 us (7%)
    all_gather x1, waiting for transfers between devices, body(): panel = lax.all_gather(amplitudes, 'blk', axis=0, tiled=True)  48.4 us
    all_to_all x1, starting transfers between devices, body(): lax.all_to_all(sent_coef, 'virt', split_axis=0, concat_axis=0, tiled=True)  5.17 us
    dot_general x1, matrix products, body(): jnp.einsum('srp,stp->rtp', columns, product, precision=lax.Precision.HIGH...  4.99 us
    all_to_all x1, starting transfers between devices, body(): lax.all_to_all(sent_tiles, 'virt', split_axis=0, concat_axis=0, tiled=True)  4.69 us
    select_n x1, other arithmetic, body(): jnp.where(filled[:, None, None], integrals[source_tile], jnp.zeros((), jn...  4.5 us
    dot_general x1, matrix products, body(): jnp.einsum('stw,pw->stp', got_tiles, panel, preferred_element_type=jnp.fl...  4.15 us
    gather x1, local copies, waits for them, and re-layouts, body(): integrals[source_tile]  2.79 us
    dot_general x1, local copies, waits for them, and re-layouts, body(): jnp.einsum('stw,pw->stp', got_tiles, panel, preferred_element_type=jnp.fl...  2.62 us
  transfers between devices with their start and end apart: 3, of which 1 were waited for; matrix products, arithmetic and copies ran while one was open for 8% of the time, Pallas kernels for 0%

commit v1 on v0

v1 whole, which is shorter than its diff:
```python
import functools

import jax
import jax.numpy as jnp
from jax import lax
from jax.experimental import pallas as pl
from jax.experimental.pallas import tpu as pltpu
from jax.sharding import PartitionSpec as P

MESH = pl.DeviceIdType.MESH


def flip(index, bits):
    step = 1
    while step <= bits:
        if bits & step:
            index = index + step * (1 - 2 * ((index // step) % 2))
        step *= 2
    return index


def kernel(
    blk_count,
    virt_count,
    tiles_hbm,
    amp_hbm,
    readers_hbm,
    slots_hbm,
    mask_hbm,
    virt_hbm,
    occ_hbm,
    first_hbm,
    second_hbm,
    out_ref,
    tiles,
    amp,
    partial,
    landed,
    denominator,
    hot,
    readers,
    slots,
    mask,
    virt_energy,
    occ,
    first,
    second,
    local_sem,
    z_send,
    z_recv,
    n_send,
    n_recv,
    sum_send,
    sum_recv,
):
    b = lax.axis_index("blk")
    v = lax.axis_index("virt")
    core = v % 2
    chip = v // 2
    kind = ((chip % 2) + ((chip // 2) % 2)) % 2
    generated = readers.shape[0]
    tile_rows = tiles.shape[0] // generated
    panel_rows, width = amp_hbm.shape
    rows = out_ref.shape[0]
    row_blocks = rows // tile_rows
    pairs = blk_count // 2

    locals_ = [
        pltpu.make_async_copy(source, target, local_sem.at[index])
        for index, (source, target) in enumerate(
            (
                (readers_hbm, readers),
                (slots_hbm, slots),
                (mask_hbm, mask),
                (virt_hbm, virt_energy),
                (occ_hbm, occ),
                (first_hbm, first),
                (second_hbm, second),
                (amp_hbm, amp.at[pl.ds(b * panel_rows, panel_rows)]),
                (tiles_hbm, tiles),
            )
        )
    ]

    barrier = pltpu.get_barrier_semaphore()
    for d in range(1, blk_count):
        pl.semaphore_signal(barrier, inc=1, device_id=(flip(b, d), v), device_id_type=MESH)
    for d in range(1, virt_count):
        pl.semaphore_signal(barrier, inc=1, device_id=(b, flip(v, d)), device_id_type=MESH)
    for copy in locals_:
        copy.start()
    pl.semaphore_wait(barrier, blk_count + virt_count - 2)

    half, quarter, eighth = width // 2, width // 4, width // 8

    def columns(core_now, kind_now):
        return pl.multiple_of(core_now * half + kind_now * quarter, quarter)

    def panel(d):
        return pl.ds(pl.multiple_of(flip(b, d) * panel_rows, panel_rows), panel_rows)

    mine = columns(core, kind)
    across = columns(core, 1 - kind)

    z_copies = {}
    for d in range(1, blk_count):
        copy = pltpu.make_async_remote_copy(
            amp_hbm.at[:, pl.ds(mine, quarter)],
            amp.at[panel(0), pl.ds(mine, quarter)],
            z_send.at[d],
            z_recv.at[d],
            device_id=(flip(b, d), v),
            device_id_type=MESH,
        )
        copy.start()
        z_copies[d] = copy

    n_copies = {}

    def share(d, which, start, size, bits):
        area = amp.at[panel(d), pl.ds(start, size)]
        copy = pltpu.make_async_remote_copy(
            area,
            area,
            n_send.at[d, which],
            n_recv.at[d, which],
            device_id=(b, flip(v, bits)),
            device_id_type=MESH,
        )
        copy.start()
        n_copies[d, which] = copy

    def spread(d):
        z_copies[d].wait_recv()
        share(d, 0, mine, eighth, 2)
        share(d, 1, pl.multiple_of(mine + eighth, eighth), eighth, 4)
        share(d, 2, mine, quarter, 1)

    def forward(d):
        n_copies[d, 0].wait_recv()
        n_copies[d, 1].wait_recv()
        share(d, 3, across, quarter, 1)

    def settle(d):
        n_copies[d, 2].wait_recv()
        n_copies[d, 3].wait_recv()

    for copy in locals_[:7]:
        copy.wait()
    all_rows = virt_count * rows
    lanes = generated * tile_rows
    lane = lax.broadcasted_iota(jnp.int32, (1, lanes), 1)
    goal = jnp.zeros((1, lanes), jnp.int32)
    for t in range(generated):
        goal = jnp.where(
            lane // tile_rows == t, (readers[t] * row_blocks + slots[t]) * tile_rows, goal
        )
    goal = goal + lane % tile_rows
    row = lax.broadcasted_iota(jnp.int32, (all_rows, lanes), 0)
    hot[...] = (row == goal).astype(jnp.float32).astype(jnp.bfloat16)

    levels = occ.shape[1]
    occ_high = occ[...].astype(jnp.bfloat16).astype(jnp.float32)
    occ_rest = occ[...] - occ_high
    occ_mid = occ_rest.astype(jnp.bfloat16).astype(jnp.float32)
    occ_low = occ_rest - occ_mid
    term = lax.broadcasted_iota(jnp.int32, (8, levels), 0)
    occ_terms = jnp.where(
        term == 0, occ_high, jnp.where(term == 1, occ_mid, jnp.where(term == 2, occ_low, 0.0))
    ).astype(jnp.bfloat16)
    count = first.shape[1]
    level = lax.broadcasted_iota(jnp.int32, (levels, count), 0)

    def energy(pair_ref):
        chosen = (level == pair_ref[...]).astype(jnp.float32).astype(jnp.bfloat16)
        terms = jnp.dot(occ_terms, chosen, preferred_element_type=jnp.float32)
        return (terms[0:1] + terms[1:2]) + terms[2:3]

    diagonal = lax.broadcasted_iota(jnp.int32, (rows, rows), 0) == lax.broadcasted_iota(
        jnp.int32, (rows, rows), 1
    )
    virt_column = jnp.sum(jnp.where(diagonal, virt_energy[...], 0.0), axis=1, keepdims=True)
    denominator[...] = (virt_column - energy(first)) - energy(second)

    sums = {}
    pair_width = 2 * panel_rows
    pair_lane = lax.broadcasted_iota(jnp.int32, (1, pair_width), 1)

    def contract(i):
        g = flip(b // 2, i)
        block = amp[pl.ds(pl.multiple_of(g * pair_width, pair_width), pair_width), :]
        product = lax.dot_general(
            tiles[...], block, (((1,), (1,)), ((), ())), preferred_element_type=jnp.float32
        )
        weight = jnp.concatenate(
            [
                jnp.broadcast_to(
                    jnp.where(pair_lane < panel_rows, mask[t, 2 * g], mask[t, 2 * g + 1]).astype(
                        jnp.float32
                    ),
                    (tile_rows, pair_width),
                )
                for t in range(generated)
            ],
            axis=0,
        )
        product = product * weight
        high = product.astype(jnp.bfloat16)
        low = (product - high.astype(jnp.float32)).astype(jnp.bfloat16)
        partial[i] = jnp.dot(hot[...], high, preferred_element_type=jnp.float32) + jnp.dot(
            hot[...], low, preferred_element_type=jnp.float32
        )
        for d in range(1, virt_count):
            peer = flip(v, d)
            copy = pltpu.make_async_remote_copy(
                partial.at[i, pl.ds(pl.multiple_of(peer * rows, rows), rows)],
                landed.at[i, d],
                sum_send.at[i, d],
                sum_recv.at[i, d],
                device_id=(b, peer),
                device_id_type=MESH,
            )
            copy.start()
            sums[i, d] = copy

    spread(1)
    forward(1)
    settle(1)
    locals_[7].wait()
    locals_[8].wait()
    contract(0)
    for i in range(1, pairs):
        spread(2 * i)
        spread(2 * i + 1)
        forward(2 * i)
        forward(2 * i + 1)
        settle(2 * i)
        settle(2 * i + 1)
        contract(i)

    for i in range(pairs):
        start = pl.multiple_of(flip(b // 2, i) * pair_width, pair_width)
        total = partial[i, pl.ds(pl.multiple_of(v * rows, rows), rows), :]
        for d in range(1, virt_count):
            sums[i, d].wait_recv()
            total = total + landed[i, d]
        out_ref[:, pl.ds(start, pair_width)] = (
            total / denominator[:, pl.ds(start, pair_width)]
        ).astype(out_ref.dtype)

    for copies in (z_copies, n_copies, sums):
        for copy in copies.values():
            copy.wait_send()


def body(
    blk_count,
    virt_count,
    integrals,
    amplitudes,
    readers,
    row_slots,
    tile_mask,
    virt_energy,
    occ_energy,
    pair_first,
    pair_second,
):
    generated, tile_rows, width = integrals.shape
    panel_rows = amplitudes.shape[0]
    rows = virt_energy.shape[0]
    columns = blk_count * panel_rows
    pairs = blk_count // 2
    levels = occ_energy.shape[0]
    anywhere = pl.BlockSpec(memory_space=pl.ANY)
    return pl.pallas_call(
        functools.partial(kernel, blk_count, virt_count),
        out_shape=jax.ShapeDtypeStruct((rows, columns), jnp.bfloat16),
        in_specs=[anywhere] * 9,
        out_specs=pl.BlockSpec(memory_space=pltpu.VMEM),
        scratch_shapes=[
            pltpu.VMEM((generated * tile_rows, width), jnp.bfloat16),
            pltpu.VMEM((columns, width), jnp.bfloat16),
            pltpu.VMEM((pairs, virt_count * rows, 2 * panel_rows), jnp.float32),
            pltpu.VMEM((pairs, virt_count, rows, 2 * panel_rows), jnp.float32),
            pltpu.VMEM((rows, columns), jnp.float32),
            pltpu.VMEM((virt_count * rows, generated * tile_rows), jnp.bfloat16),
            pltpu.SMEM((generated,), jnp.int32),
            pltpu.SMEM((generated,), jnp.int32),
            pltpu.SMEM((generated, blk_count), jnp.int32),
            pltpu.VMEM((1, rows), jnp.float32),
            pltpu.VMEM((1, levels), jnp.float32),
            pltpu.VMEM((1, columns), jnp.int32),
            pltpu.VMEM((1, columns), jnp.int32),
            pltpu.SemaphoreType.DMA((9,)),
            pltpu.SemaphoreType.DMA((blk_count,)),
            pltpu.SemaphoreType.DMA((blk_count,)),
            pltpu.SemaphoreType.DMA((blk_count, 4)),
            pltpu.SemaphoreType.DMA((blk_count, 4)),
            pltpu.SemaphoreType.DMA((pairs, virt_count)),
            pltpu.SemaphoreType.DMA((pairs, virt_count)),
        ],
        compiler_params=pltpu.CompilerParams(
            collective_id=0, has_side_effects=True, vmem_limit_bytes=48 * 1024 * 1024
        ),
        name="ladder",
    )(
        integrals.reshape(generated * tile_rows, width),
        amplitudes,
        readers,
        row_slots,
        tile_mask,
        virt_energy.reshape(1, rows),
        occ_energy.reshape(1, levels),
        pair_first.reshape(1, columns),
        pair_second.reshape(1, columns),
    )


def solution(mesh):
    placed = (
        P(("blk", "virt"), None, None),
        P("blk", None),
        P(("blk", "virt")),
        P(("blk", "virt")),
        P(("blk", "virt"), None),
        P(("blk", "virt")),
        P(),
        P(),
        P(),
    )
    return jax.shard_map(
        functools.partial(body, mesh.shape["blk"], mesh.shape["virt"]),
        mesh=mesh,
        in_specs=placed,
        out_specs=P(("blk", "virt"), None),
        check_vma=False,
    )
```

time: 98.4 us -> 42.3 us (0.43)
  waiting for transfers between devices: 49.1 us -> 0 us
  Pallas kernels: 0 us -> 34 us
  between operations: 13.5 us -> 0.02 us
  starting transfers between devices: 9.9 us -> 0 us
  other arithmetic: 9.47 us -> 0 us
  matrix products: 9.28 us -> 0 us
  local copies, waits for them, and re-layouts: 6.7 us -> 8.03 us
    all_gather x1 -> x0, waiting for transfers between devices: 48.4 us -> none  [body(): panel = lax.all_gather(amplitudes, 'blk', axis=0, tiled=True)]
    pallas_call x0 -> x1, Pallas kernels: none -> 34 us  [body(): pl.pallas_call(functools.partial(kernel, blk_count, virt_count), out_shap...]
    all_to_all x2 -> x0, starting transfers between devices: 9.86 us -> none  [the longest x1 5.17 us: body(): lax.all_to_all(sent_coef, 'virt', split_axis=0, concat_axis=0, tiled=True)]
    dot_general x3 -> x0, matrix products: 9.28 us -> none  [the longest x1 4.99 us: body(): jnp.einsum('srp,stp->rtp', columns, product, precision=lax.Precision.HIGH...]
    unnamed x10 -> x16, local copies, waits for them, and re-layouts: 0.02 us -> 7.33 us
    select_n x3 -> x0, other arithmetic: 4.51 us -> none  [the longest x1 4.5 us: body(): jnp.where(filled[:, None, None], integrals[source_tile], jnp.zeros((), jn...]
    gather x2 -> x0, local copies, waits for them, and re-layouts: 3.39 us -> none  [the longest x1 2.79 us: body(): integrals[source_tile]]
    dot_general x2 -> x0, local copies, waits for them, and re-layouts: 2.86 us -> none  [the longest x1 2.62 us: body(): jnp.einsum('stw,pw->stp', got_tiles, panel, preferred_element_type=jnp.fl...]
  transfers between devices with their start and end apart: 3 -> 0, of which waited for: 1 -> 0; matrix products, arithmetic and copies ran while one was open for 8% -> 0% of each run, Pallas kernels for 0% -> 0%
where the time goes in v1:
time: 42.3 us; the launch traced here: 42 us
  Pallas kernels  34 us (80%)
  local copies, waits for them, and re-layouts  8.03 us (19%)
    pallas_call x1, Pallas kernels, body(): pl.pallas_call(functools.partial(kernel, blk_count, virt_count), out_shap...  34 us
    unnamed x16, local copies, waits for them, and re-layouts  7.33 us

profile of v1, /device:TPU:0, one launch (start us, length us, event | category | flops | bytes accessed | tf_op | source)
XLA Modules:
  0.0 42.0 jit_solution(12384806949569542434)
XLA Ops:
  0.0 0.7 %reshape.17.occ_hbm = f32[1,1200]{1,0:T(1,128)S(1)} reshape(f32[1200]{0:T(1024)} %param.15) | data formatting | bytes 9600 | tf_op jit(solution)/shard_map/reshape | solution.py:314
  0.7 0.8 %copy.10.mask_hbm = s32[16,4]{1,0:T(8,128)S(1)} copy(s32[16,4]{0,1:T(4,128)} %param.13) | data formatting | bytes 512 | tf_op args[4]
  1.5 0.0 copy-start
  1.5 1.6 %copy-done = bf16[16,16,4096]{2,1,0:T(8,128)(2,1)S(1)} copy-done((bf16[16,16,4096]{2,1,0:T(8,128)(2,1)S(1)}, bf16[16,16,4096]{2,1,0:T(8,128)(2,1)}, u32[]{:S(2)}) %copy-start) | copy-done | bytes 2097176
  3.1 0.0 copy-start.1
  3.1 1.0 %copy-done.1 = bf16[64,4096]{1,0:T(8,128)(2,1)S(1)} copy-done((bf16[64,4096]{1,0:T(8,128)(2,1)S(1)}, bf16[64,4096]{1,0:T(8,128)(2,1)}, u32[]{:S(2)}) %copy-start.1) | copy-done | bytes 524312
  4.1 0.0 copy-start.2
  4.1 0.7 %copy-done.2 = s32[256]{0:T(256)S(1)} copy-done((s32[256]{0:T(256)S(1)}, s32[256]{0:T(256)}, u32[]{:S(2)}) %copy-start.2) | copy-done | bytes 1048
  4.8 0.0 copy-start.3
  4.8 0.7 %copy-done.3 = s32[256]{0:T(256)S(1)} copy-done((s32[256]{0:T(256)S(1)}, s32[256]{0:T(256)}, u32[]{:S(2)}) %copy-start.3) | copy-done | bytes 1048
  5.5 0.0 copy-start.4
  5.5 0.7 %copy-done.4 = s32[16]{0:T(128)S(1)} copy-done((s32[16]{0:T(128)S(1)}, s32[16]{0:T(128)}, u32[]{:S(2)}) %copy-start.4) | copy-done | bytes 88
  6.1 0.0 copy-start.5
  6.1 0.7 %copy-done.5 = s32[16]{0:T(128)S(1)} copy-done((s32[16]{0:T(128)S(1)}, s32[16]{0:T(128)}, u32[]{:S(2)}) %copy-start.5) | copy-done | bytes 88
  6.8 0.0 copy-start.6
  6.8 0.7 %copy-done.6 = f32[64]{0:T(128)S(1)} copy-done((f32[64]{0:T(128)S(1)}, f32[64]{0:T(128)}, u32[]{:S(2)}) %copy-start.6) | copy-done | bytes 280
  7.4 34.0 %ladder.1 = bf16[64,256]{1,0:T(8,128)(2,1)S(1)} custom-call(bf16[256,4096]{1,0:T(8,128)(2,1)S(1)} %bitcast.4, bf16[64,4096]{1,0:T(8,128)(2,1)S(1)} %copy-done.1, s32[16]{0:T(128)S(1)} %copy-done.4, s32[16]{0:T(128)S(1)} %copy-done.5, s32[16,4]{1,0:T(8,128)S(1)} %copy.10.mask_hbm, f32[1,64]{1,0:T(1,128)S(1)} %bitcast.7, f32[1,1200]{1,0:T(1,128)S(1)} %reshape.17.occ_hbm, ...), custom_call_target="tpu_custom_call" | custom-call | tf_op jit(solution)/shard_map/ladder/pallas_call | solution.py:276
  41.4 0.6 %copy.12 = bf16[64,256]{1,0:T(8,128)(2,1)} copy(bf16[64,256]{1,0:T(8,128)(2,1)S(1)} %ladder.1) | data formatting | bytes 65536
Async XLA Ops:
  1.5 1.6 %copy-start = (bf16[16,16,4096]{2,1,0:T(8,128)(2,1)S(1)}, bf16[16,16,4096]{2,1,0:T(8,128)(2,1)}, u32[]{:S(2)}) copy-start(bf16[16,16,4096]{2,1,0:T(8,128)(2,1)} %param.9) | copy-start | bytes 6291460
  3.1 1.0 %copy-start.1 = (bf16[64,4096]{1,0:T(8,128)(2,1)S(1)}, bf16[64,4096]{1,0:T(8,128)(2,1)}, u32[]{:S(2)}) copy-start(bf16[64,4096]{1,0:T(8,128)(2,1)} %amp_hbm.1) | copy-start | bytes 1572868
  4.1 0.7 %copy-start.2 = (s32[256]{0:T(256)S(1)}, s32[256]{0:T(256)}, u32[]{:S(2)}) copy-start(s32[256]{0:T(256)} %param.16) | copy-start | bytes 3076
  4.8 0.7 %copy-start.3 = (s32[256]{0:T(256)S(1)}, s32[256]{0:T(256)}, u32[]{:S(2)}) copy-start(s32[256]{0:T(256)} %param.17) | copy-start | bytes 3076
  5.5 0.7 %copy-start.4 = (s32[16]{0:T(128)S(1)}, s32[16]{0:T(128)}, u32[]{:S(2)}) copy-start(s32[16]{0:T(128)} %readers_hbm.1) | copy-start | bytes 196
  6.1 0.7 %copy-start.5 = (s32[16]{0:T(128)S(1)}, s32[16]{0:T(128)}, u32[]{:S(2)}) copy-start(s32[16]{0:T(128)} %slots_hbm.1) | copy-start | bytes 196
  6.8 0.7 %copy-start.6 = (f32[64]{0:T(128)S(1)}, f32[64]{0:T(128)}, u32[]{:S(2)}) copy-start(f32[64]{0:T(128)} %param.14) | copy-start | bytes 772

commit v2 on v1

--- a/solution.py
+++ b/solution.py
@@ -35,6 +35,7 @@
     tiles,
     amp,
     partial,
+    swapped,
     landed,
     denominator,
     hot,
@@ -91,22 +92,25 @@
         copy.start()
     pl.semaphore_wait(barrier, blk_count + virt_count - 2)
 
-    half, quarter, eighth = width // 2, width // 4, width // 8
-
-    def columns(core_now, kind_now):
-        return pl.multiple_of(core_now * half + kind_now * quarter, quarter)
+    half, piece = width // 2, width // 8
+    spot = chip % 4
+
+    def columns(core_now, spot_now):
+        return pl.multiple_of(core_now * half + spot_now * piece, piece)
 
     def panel(d):
         return pl.ds(pl.multiple_of(flip(b, d) * panel_rows, panel_rows), panel_rows)
 
-    mine = columns(core, kind)
-    across = columns(core, 1 - kind)
+    mine = columns(core, spot)
+    beside_x = columns(core, flip(spot, 1))
+    beside_y = columns(core, flip(spot, 2))
+    opposite = columns(core, flip(spot, 3))
 
     z_copies = {}
     for d in range(1, blk_count):
         copy = pltpu.make_async_remote_copy(
-            amp_hbm.at[:, pl.ds(mine, quarter)],
-            amp.at[panel(0), pl.ds(mine, quarter)],
+            amp_hbm.at[:, pl.ds(mine, piece)],
+            amp.at[panel(0), pl.ds(mine, piece)],
             z_send.at[d],
             z_recv.at[d],
             device_id=(flip(b, d), v),
@@ -132,36 +136,46 @@
 
     def spread(d):
         z_copies[d].wait_recv()
-        share(d, 0, mine, eighth, 2)
-        share(d, 1, pl.multiple_of(mine + eighth, eighth), eighth, 4)
-        share(d, 2, mine, quarter, 1)
-
-    def forward(d):
+        share(d, 0, mine, piece, 2)
+        share(d, 1, mine, piece, 4)
+        share(d, 2, mine, piece, 1)
+
+    def relay(d):
         n_copies[d, 0].wait_recv()
+        share(d, 3, beside_x, piece // 2, 4)
         n_copies[d, 1].wait_recv()
-        share(d, 3, across, quarter, 1)
+        share(d, 4, pl.multiple_of(beside_y + piece // 2, piece // 2), piece // 2, 2)
+        share(d, 5, beside_x, piece, 1)
+        share(d, 6, beside_y, piece, 1)
+
+    def finish(d):
+        n_copies[d, 3].wait_recv()
+        n_copies[d, 4].wait_recv()
+        share(d, 7, opposite, piece, 1)
 
     def settle(d):
-        n_copies[d, 2].wait_recv()
-        n_copies[d, 3].wait_recv()
+        for which in (2, 5, 6, 7):
+            n_copies[d, which].wait_recv()
 
     for copy in locals_[:7]:
         copy.wait()
+    chips = virt_count // 2
     all_rows = virt_count * rows
+    core_rows = chips * rows
     lanes = generated * tile_rows
     lane = lax.broadcasted_iota(jnp.int32, (1, lanes), 1)
     goal = jnp.zeros((1, lanes), jnp.int32)
     for t in range(generated):
-        goal = jnp.where(
-            lane // tile_rows == t, (readers[t] * row_blocks + slots[t]) * tile_rows, goal
-        )
+        place = (readers[t] % 2) * chips + readers[t] // 2
+        goal = jnp.where(lane // tile_rows == t, (place * row_blocks + slots[t]) * tile_rows, goal)
     goal = goal + lane % tile_rows
     row = lax.broadcasted_iota(jnp.int32, (all_rows, lanes), 0)
     hot[...] = (row == goal).astype(jnp.float32).astype(jnp.bfloat16)
 
-    levels = occ.shape[1]
-    occ_high = occ[...].astype(jnp.bfloat16).astype(jnp.float32)
-    occ_rest = occ[...] - occ_high
+    levels = occ.shape[0]
+    occ_row = occ[...].reshape(1, levels)
+    occ_high = occ_row.astype(jnp.bfloat16).astype(jnp.float32)
+    occ_rest = occ_row - occ_high
     occ_mid = occ_rest.astype(jnp.bfloat16).astype(jnp.float32)
     occ_low = occ_rest - occ_mid
     term = lax.broadcasted_iota(jnp.int32, (8, levels), 0)
@@ -195,7 +209,7 @@
         weight = jnp.concatenate(
             [
                 jnp.broadcast_to(
-                    jnp.where(pair_lane < panel_rows, mask[t, 2 * g], mask[t, 2 * g + 1]).astype(
+                    jnp.where(pair_lane < panel_rows, mask[2 * g, t], mask[2 * g + 1, t]).astype(
                         jnp.float32
                     ),
                     (tile_rows, pair_width),
@@ -210,38 +224,62 @@
         partial[i] = jnp.dot(hot[...], high, preferred_element_type=jnp.float32) + jnp.dot(
             hot[...], low, preferred_element_type=jnp.float32
         )
-        for d in range(1, virt_count):
-            peer = flip(v, d)
+        copy = pltpu.make_async_remote_copy(
+            partial.at[i, pl.ds(pl.multiple_of((1 - core) * core_rows, core_rows), core_rows)],
+            swapped.at[i],
+            sum_send.at[i, 0],
+            sum_recv.at[i, 0],
+            device_id=(b, flip(v, 1)),
+            device_id_type=MESH,
+        )
+        copy.start()
+        sums[i, 0] = copy
+
+    def scatter(i):
+        own = pl.ds(pl.multiple_of(core * core_rows, core_rows), core_rows)
+        sums[i, 0].wait_recv()
+        swapped[i] = swapped[i] + partial[i, own, :]
+        for d in range(1, chips):
+            peer = flip(chip, d)
             copy = pltpu.make_async_remote_copy(
-                partial.at[i, pl.ds(pl.multiple_of(peer * rows, rows), rows)],
+                swapped.at[i, pl.ds(pl.multiple_of(peer * rows, rows), rows)],
                 landed.at[i, d],
                 sum_send.at[i, d],
                 sum_recv.at[i, d],
-                device_id=(b, peer),
+                device_id=(b, flip(v, 2 * d)),
                 device_id_type=MESH,
             )
             copy.start()
             sums[i, d] = copy
 
-    spread(1)
-    forward(1)
-    settle(1)
     locals_[7].wait()
     locals_[8].wait()
-    contract(0)
     for i in range(1, pairs):
+        if i == 1:
+            spread(1)
         spread(2 * i)
+        if i == 1:
+            relay(1)
         spread(2 * i + 1)
-        forward(2 * i)
-        forward(2 * i + 1)
+        if i == 1:
+            finish(1)
+            settle(1)
+        relay(2 * i)
+        relay(2 * i + 1)
+        if i == 1:
+            contract(0)
+            scatter(0)
+        finish(2 * i)
+        finish(2 * i + 1)
         settle(2 * i)
         settle(2 * i + 1)
         contract(i)
+        scatter(i)
 
     for i in range(pairs):
         start = pl.multiple_of(flip(b // 2, i) * pair_width, pair_width)
-        total = partial[i, pl.ds(pl.multiple_of(v * rows, rows), rows), :]
-        for d in range(1, virt_count):
+        total = swapped[i, pl.ds(pl.multiple_of(chip * rows, rows), rows), :]
+        for d in range(1, chips):
             sums[i, d].wait_recv()
             total = total + landed[i, d]
         out_ref[:, pl.ds(start, pair_width)] = (
@@ -282,26 +320,27 @@
             pltpu.VMEM((generated * tile_rows, width), jnp.bfloat16),
             pltpu.VMEM((columns, width), jnp.bfloat16),
             pltpu.VMEM((pairs, virt_count * rows, 2 * panel_rows), jnp.float32),
-            pltpu.VMEM((pairs, virt_count, rows, 2 * panel_rows), jnp.float32),
+            pltpu.VMEM((pairs, virt_count // 2 * rows, 2 * panel_rows), jnp.float32),
+            pltpu.VMEM((pairs, virt_count // 2, rows, 2 * panel_rows), jnp.float32),
             pltpu.VMEM((rows, columns), jnp.float32),
             pltpu.VMEM((virt_count * rows, generated * tile_rows), jnp.bfloat16),
             pltpu.SMEM((generated,), jnp.int32),
             pltpu.SMEM((generated,), jnp.int32),
-            pltpu.SMEM((generated, blk_count), jnp.int32),
+            pltpu.SMEM((blk_count, generated), jnp.int32),
             pltpu.VMEM((1, rows), jnp.float32),
-            pltpu.VMEM((1, levels), jnp.float32),
+            pltpu.VMEM((levels,), jnp.float32),
             pltpu.VMEM((1, columns), jnp.int32),
             pltpu.VMEM((1, columns), jnp.int32),
             pltpu.SemaphoreType.DMA((9,)),
             pltpu.SemaphoreType.DMA((blk_count,)),
             pltpu.SemaphoreType.DMA((blk_count,)),
-            pltpu.SemaphoreType.DMA((blk_count, 4)),
-            pltpu.SemaphoreType.DMA((blk_count, 4)),
-            pltpu.SemaphoreType.DMA((pairs, virt_count)),
-            pltpu.SemaphoreType.DMA((pairs, virt_count)),
+            pltpu.SemaphoreType.DMA((blk_count, 8)),
+            pltpu.SemaphoreType.DMA((blk_count, 8)),
+            pltpu.SemaphoreType.DMA((pairs, virt_count // 2)),
+            pltpu.SemaphoreType.DMA((pairs, virt_count // 2)),
         ],
         compiler_params=pltpu.CompilerParams(
-            collective_id=0, has_side_effects=True, vmem_limit_bytes=48 * 1024 * 1024
+            collective_id=0, has_side_effects=True, vmem_limit_bytes=60 * 1024 * 1024
         ),
         name="ladder",
     )(
@@ -309,9 +348,9 @@
         amplitudes,
         readers,
         row_slots,
-        tile_mask,
+        tile_mask.T,
         virt_energy.reshape(1, rows),
-        occ_energy.reshape(1, levels),
+        occ_energy,
         pair_first.reshape(1, columns),
         pair_second.reshape(1, columns),
     )

time: 42.3 us -> 30.6 us (0.72)
  local copies, waits for them, and re-layouts: 8.03 us -> 1.38 us
  Pallas kernels: 34 us -> 29 us
    unnamed x16 -> x1, local copies, waits for them, and re-layouts: 7.33 us -> 1.38 us
    pallas_call x1, Pallas kernels: 34 us -> 29 us  [body(): pl.pallas_call(functools.partial(kernel, blk_count, virt_count), out_shap...]
    reshape x1 -> x0, local copies, waits for them, and re-layouts: 0.7 us -> none  [body(): occ_energy.reshape(1, levels)]
where the time goes in v2:
time: 30.6 us; the launch traced here: 30.4 us
  Pallas kernels  29 us (95%)
  local copies, waits for them, and re-layouts  1.38 us (5%)
    pallas_call x1, Pallas kernels, body(): pl.pallas_call(functools.partial(kernel, blk_count, virt_count), out_shap...  29 us
    unnamed x1, local copies, waits for them, and re-layouts  1.38 us

profile of v2, /device:TPU:0, one launch (start us, length us, event | category | flops | bytes accessed | tf_op | source)
XLA Modules:
  0.0 30.4 jit_solution(10218457551443530755)
XLA Ops:
  0.0 29.0 %ladder.1 = bf16[64,256]{1,0:T(8,128)(2,1)} custom-call(bf16[256,4096]{1,0:T(8,128)(2,1)} %bitcast.5, bf16[64,4096]{1,0:T(8,128)(2,1)} %amp_hbm.1, s32[16]{0:T(128)} %readers_hbm.1, s32[16]{0:T(128)} %slots_hbm.1, s32[4,16]{1,0:T(4,128)} %bitcast.6, f32[1,64]{1,0:T(1,128)} %bitcast.9, f32[1200]{0:T(1024)} %occ_hbm.1, s32[1,256]{1,0:T(1,128)} %bitcast.7, ...), custom_call_target="tpu_custom_call" | custom-call | tf_op jit(solution)/shard_map/ladder/pallas_call | solution.py:314
  29.0 1.4 %copy.11 = bf16[64,256]{1,0:T(8,128)(2,1)} copy(bf16[64,256]{1,0:T(8,128)(2,1)} %ladder.1) | data formatting | bytes 65536

commit v3 on v2

--- a/solution.py
+++ b/solution.py
@@ -34,6 +34,8 @@
     out_ref,
     tiles,
     amp,
+    products,
+    weights,
     partial,
     swapped,
     landed,
@@ -138,23 +140,28 @@
         z_copies[d].wait_recv()
         share(d, 0, mine, piece, 2)
         share(d, 1, mine, piece, 4)
+        if d == 1:
+            share(d, 3, mine, piece, 6)
         share(d, 2, mine, piece, 1)
 
     def relay(d):
         n_copies[d, 0].wait_recv()
-        share(d, 3, beside_x, piece // 2, 4)
+        if not d == 1:
+            share(d, 3, beside_x, piece // 2, 4)
         n_copies[d, 1].wait_recv()
-        share(d, 4, pl.multiple_of(beside_y + piece // 2, piece // 2), piece // 2, 2)
+        if not d == 1:
+            share(d, 4, pl.multiple_of(beside_y + piece // 2, piece // 2), piece // 2, 2)
         share(d, 5, beside_x, piece, 1)
         share(d, 6, beside_y, piece, 1)
 
     def finish(d):
         n_copies[d, 3].wait_recv()
-        n_copies[d, 4].wait_recv()
+        if not d == 1:
+            n_copies[d, 4].wait_recv()
         share(d, 7, opposite, piece, 1)
 
-    def settle(d):
-        for which in (2, 5, 6, 7):
+    def settle(which, *panels):
+        for d in panels:
             n_copies[d, which].wait_recv()
 
     for copy in locals_[:7]:
@@ -200,13 +207,23 @@
     pair_width = 2 * panel_rows
     pair_lane = lax.broadcasted_iota(jnp.int32, (1, pair_width), 1)
 
-    def contract(i):
+    def multiply(i, spot_now, begin=False):
+        rows_now = pl.ds(pl.multiple_of(flip(b // 2, i) * pair_width, pair_width), pair_width)
+        total = None if begin else products[i]
+        for core_now in range(2):
+            depth = pl.ds(columns(core_now, spot_now), piece)
+            term = lax.dot_general(
+                tiles[:, depth],
+                amp[rows_now, depth],
+                (((1,), (1,)), ((), ())),
+                preferred_element_type=jnp.float32,
+            )
+            total = term if total is None else total + term
+        products[i] = total
+
+    for i in range(pairs):
         g = flip(b // 2, i)
-        block = amp[pl.ds(pl.multiple_of(g * pair_width, pair_width), pair_width), :]
-        product = lax.dot_general(
-            tiles[...], block, (((1,), (1,)), ((), ())), preferred_element_type=jnp.float32
-        )
-        weight = jnp.concatenate(
+        weights[i] = jnp.concatenate(
             [
                 jnp.broadcast_to(
                     jnp.where(pair_lane < panel_rows, mask[2 * g, t], mask[2 * g + 1, t]).astype(
@@ -218,12 +235,20 @@
             ],
             axis=0,
         )
-        product = product * weight
+
+    def contract(i):
+        product = products[i]
+        product = product * weights[i]
         high = product.astype(jnp.bfloat16)
         low = (product - high.astype(jnp.float32)).astype(jnp.bfloat16)
-        partial[i] = jnp.dot(hot[...], high, preferred_element_type=jnp.float32) + jnp.dot(
-            hot[...], low, preferred_element_type=jnp.float32
-        )
+        terms = jnp.concatenate([high, low], axis=1)
+
+        def gather_rows(core_now):
+            area = pl.ds(pl.multiple_of(core_now * core_rows, core_rows), core_rows)
+            both = jnp.dot(hot[area, :], terms, preferred_element_type=jnp.float32)
+            partial[i, area, :] = both[:, :pair_width] + both[:, pair_width:]
+
+        gather_rows(1 - core)
         copy = pltpu.make_async_remote_copy(
             partial.at[i, pl.ds(pl.multiple_of((1 - core) * core_rows, core_rows), core_rows)],
             swapped.at[i],
@@ -234,15 +259,19 @@
         )
         copy.start()
         sums[i, 0] = copy
+        gather_rows(core)
 
     def scatter(i):
-        own = pl.ds(pl.multiple_of(core * core_rows, core_rows), core_rows)
         sums[i, 0].wait_recv()
-        swapped[i] = swapped[i] + partial[i, own, :]
-        for d in range(1, chips):
+        for d in (3, 1, 2) + tuple(range(4, chips)) + (0,):
             peer = flip(chip, d)
+            area = pl.ds(pl.multiple_of(peer * rows, rows), rows)
+            own = pl.ds(pl.multiple_of(core * core_rows + peer * rows, rows), rows)
+            swapped[i, area, :] = swapped[i, area, :] + partial[i, own, :]
+            if d == 0:
+                continue
             copy = pltpu.make_async_remote_copy(
-                swapped.at[i, pl.ds(pl.multiple_of(peer * rows, rows), rows)],
+                swapped.at[i, area],
                 landed.at[i, d],
                 sum_send.at[i, d],
                 sum_recv.at[i, d],
@@ -254,25 +283,33 @@
 
     locals_[7].wait()
     locals_[8].wait()
+
+    def gathered(i, step, *panels):
+        settle((2, 5, 6, 7)[step], *panels)
+        multiply(i, flip(spot, step), step == 0)
+
     for i in range(1, pairs):
+        even, odd = 2 * i, 2 * i + 1
         if i == 1:
             spread(1)
-        spread(2 * i)
+        spread(even)
+        spread(odd)
         if i == 1:
             relay(1)
-        spread(2 * i + 1)
+            finish(1)
+            for step in range(3):
+                gathered(0, step, 1)
+        relay(even)
+        relay(odd)
         if i == 1:
-            finish(1)
-            settle(1)
-        relay(2 * i)
-        relay(2 * i + 1)
-        if i == 1:
+            gathered(0, 3, 1)
             contract(0)
             scatter(0)
-        finish(2 * i)
-        finish(2 * i + 1)
-        settle(2 * i)
-        settle(2 * i + 1)
+        for step in range(3):
+            gathered(i, step, even, odd)
+        finish(even)
+        finish(odd)
+        gathered(i, 3, even, odd)
         contract(i)
         scatter(i)
 
@@ -319,6 +356,8 @@
         scratch_shapes=[
             pltpu.VMEM((generated * tile_rows, width), jnp.bfloat16),
             pltpu.VMEM((columns, width), jnp.bfloat16),
+            pltpu.VMEM((pairs, generated * tile_rows, 2 * panel_rows), jnp.float32),
+            pltpu.VMEM((pairs, generated * tile_rows, 2 * panel_rows), jnp.float32),
             pltpu.VMEM((pairs, virt_count * rows, 2 * panel_rows), jnp.float32),
             pltpu.VMEM((pairs, virt_count // 2 * rows, 2 * panel_rows), jnp.float32),
             pltpu.VMEM((pairs, virt_count // 2, rows, 2 * panel_rows), jnp.float32),

time: 30.6 us -> 29.1 us (0.951)
  Pallas kernels: 29 us -> 27.6 us
    pallas_call x1, Pallas kernels: 29 us -> 27.6 us  [body(): pl.pallas_call(functools.partial(kernel, blk_count, virt_count), out_shap...]
where the time goes in v3:
time: 29.1 us; the launch traced here: 28.9 us
  Pallas kernels  27.6 us (95%)
  local copies, waits for them, and re-layouts  1.38 us (5%)
    pallas_call x1, Pallas kernels, body(): pl.pallas_call(functools.partial(kernel, blk_count, virt_count), out_shap...  27.6 us
    unnamed x1, local copies, waits for them, and re-layouts  1.38 us

profile of v3, /device:TPU:0, one launch (start us, length us, event | category | flops | bytes accessed | tf_op | source)
XLA Modules:
  0.0 28.9 jit_solution(16360080515306501209)
XLA Ops:
  0.0 27.6 %ladder.1 = bf16[64,256]{1,0:T(8,128)(2,1)} custom-call(bf16[256,4096]{1,0:T(8,128)(2,1)} %bitcast.5, bf16[64,4096]{1,0:T(8,128)(2,1)} %amp_hbm.1, s32[16]{0:T(128)} %readers_hbm.1, s32[16]{0:T(128)} %slots_hbm.1, s32[4,16]{1,0:T(4,128)} %bitcast.6, f32[1,64]{1,0:T(1,128)} %bitcast.9, f32[1200]{0:T(1024)} %occ_hbm.1, s32[1,256]{1,0:T(1,128)} %bitcast.7, ...), custom_call_target="tpu_custom_call" | custom-call | tf_op jit(solution)/shard_map/ladder/pallas_call | solution.py:351
  27.6 1.4 %copy.11 = bf16[64,256]{1,0:T(8,128)(2,1)} copy(bf16[64,256]{1,0:T(8,128)(2,1)} %ladder.1) | data formatting | bytes 65536

commit v4 on v3

--- a/solution.py
+++ b/solution.py
@@ -109,7 +109,7 @@
     opposite = columns(core, flip(spot, 3))
 
     z_copies = {}
-    for d in range(1, blk_count):
+    for d in tuple(range(2, blk_count)) + (1,):
         copy = pltpu.make_async_remote_copy(
             amp_hbm.at[:, pl.ds(mine, piece)],
             amp.at[panel(0), pl.ds(mine, piece)],
@@ -304,11 +304,12 @@
         if i == 1:
             gathered(0, 3, 1)
             contract(0)
-            scatter(0)
         for step in range(3):
             gathered(i, step, even, odd)
         finish(even)
         finish(odd)
+        if i == 1:
+            scatter(0)
         gathered(i, 3, even, odd)
         contract(i)
         scatter(i)

time: 29.1 us -> 28.8 us (0.990)
  Pallas kernels: 27.6 us -> 27.2 us
    pallas_call x1, Pallas kernels: 27.6 us -> 27.2 us  [body(): pl.pallas_call(functools.partial(kernel, blk_count, virt_count), out_shap...]
where the time goes in v4:
time: 28.8 us; the launch traced here: 28.6 us
  Pallas kernels  27.2 us (94%)
  local copies, waits for them, and re-layouts  1.38 us (5%)
    pallas_call x1, Pallas kernels, body(): pl.pallas_call(functools.partial(kernel, blk_count, virt_count), out_shap...  27.2 us
    unnamed x1, local copies, waits for them, and re-layouts  1.38 us

profile of v4, /device:TPU:0, one launch (start us, length us, event | category | flops | bytes accessed | tf_op | source)
XLA Modules:
  0.0 28.6 jit_solution(5953338282189739369)
XLA Ops:
  0.0 27.2 %ladder.1 = bf16[64,256]{1,0:T(8,128)(2,1)} custom-call(bf16[256,4096]{1,0:T(8,128)(2,1)} %bitcast.5, bf16[64,4096]{1,0:T(8,128)(2,1)} %amp_hbm.1, s32[16]{0:T(128)} %readers_hbm.1, s32[16]{0:T(128)} %slots_hbm.1, s32[4,16]{1,0:T(4,128)} %bitcast.6, f32[1,64]{1,0:T(1,128)} %bitcast.9, f32[1200]{0:T(1024)} %occ_hbm.1, s32[1,256]{1,0:T(1,128)} %bitcast.7, ...), custom_call_target="tpu_custom_call" | custom-call | tf_op jit(solution)/shard_map/ladder/pallas_call | solution.py:352
  27.2 1.4 %copy.11 = bf16[64,256]{1,0:T(8,128)(2,1)} copy(bf16[64,256]{1,0:T(8,128)(2,1)} %ladder.1) | data formatting | bytes 65536
